TPU v7x, 32 devices: a whole 2x2x4 slice. The times are simulated.
32 devices in a mesh: groups: 2 (over y), space: 8 (over z, x), dp: 2 (over core).
Axes of the slice: x: 2, y: 2, z: 4, core: 2. Of those that a mesh axis runs over, the one named last changes fastest.
Arguments:
- features: bfloat16 [4, 16, 8, 8, 512], P(('groups', 'dp'), 'space'), parts along dimension 0, may hold values from -6 to 6
- cotangent: bfloat16 [4, 16, 8, 8, 512], P(('groups', 'dp'), 'space'), parts along dimension 0, may hold values from -6 to 6
- kernel: bfloat16 [3, 3, 3, 64, 64], replicated, may hold values from -0.15625 to 0.15625
- neighbours: int32 [4, 16, 6], P(('groups', 'dp'), 'space'), parts along dimension 0, may hold values from -1 to 15, as said below
Outputs:
- response: bfloat16 [4, 16, 8, 8, 512], P(('groups', 'dp'), 'space'), parts along dimension 0
- feature_grad: bfloat16 [4, 16, 8, 8, 512], P(('groups', 'dp'), 'space'), parts along dimension 0
- kernel_grad: float32 [6, 3, 3, 64, 64], P('groups'), parts along dimension 0
There are 2 independent parts, one for each index of `groups`. A program takes and returns all parts, laid end to end along the dimension named above; an argument that names none is the same for every part. Nothing has to cross between parts.
Inputs may be any that keep to these rules, and one draw needn't show every extreme that they name: `neighbours`: the active bricks lie on a lattice of 3 by 8 by 4 bricks. Tile t sits at position p = t + 2: it covers lattice row p // 4 of the first dimension, rows 2 * (p % 4) to 2 * (p % 4) + 1 of the second and all rows of the third; it holds exactly 2 active bricks, in slots 2 * t to 2 * t + 1, listed by second then third lattice coordinate. In each realization one third-dimension row z is drawn, and every tile holds the bricks at z in its first and in its last second-dimension row; its other bricks are drawn at random. Directions are first dimension down, up, second down, up, third down, up; the relation is symmetric (if brick u is the up neighbour of s, s is the down neighbour of u), and -1 marks a neighbour that is inactive or outside the lattice.
All inputs are finite; a program needn't handle non-finite values.
Results may differ from a plain program's by a relative error of at most 0.0045.
Values may be sent and summed in bfloat16 or wider, within the bound.
No kernel may reach another device: no remote copies, remote signals or barrier semaphores. Data moves between devices by JAX's collectives and lax.ppermute only.
A program may use at most 64 MiB of HBM per device.

v0:
```python
import math
import jax
import jax.numpy as jnp
from jax import lax
from jax.sharding import PartitionSpec as P

TILES_Y = 4


def shifted(x, axis, by):
    count = lax.axis_size(axis)
    pairs = [(i, i + by) for i in range(count) if 0 <= i + by < count]
    return lax.ppermute(x, axis, pairs)


def choose_rows(tables, shifts, column, source_device, flat_slot, present, position):
    stacked = jnp.concatenate(tables, axis=0)
    row_count = tables[0].shape[0]
    source_pick = jnp.zeros_like(flat_slot[:, column])
    for number, offset in enumerate(shifts):
        source_pick = jnp.where(source_device[:, column] == position + offset, number, source_pick)
    row_index = source_pick * row_count + flat_slot[:, column]
    picked = jnp.take(stacked, row_index, axis=0)
    present_rows = present[:, column].reshape((-1,) + (1,) * (picked.ndim - 1))
    return jnp.where(present_rows, picked, jnp.zeros_like(picked))


def make_banded(weights, channels):
    toeplitz = jnp.zeros((3, 3, 4, channels, 2, channels), jnp.bfloat16)
    for out_cell in range(2):
        for tap_z in range(3):
            toeplitz = toeplitz.at[:, :, out_cell + tap_z, :, out_cell, :].set(weights[:, :, tap_z])
    return toeplitz.reshape(3, 3, 4 * channels, 2 * channels)


def make_windows(extended, channels, pairs_z):
    return jnp.stack(
        [
            extended[..., 2 * channels * block_index : 2 * channels * block_index + 4 * channels]
            for block_index in range(pairs_z)
        ],
        axis=3,
    )


def correlate(windows, banded, rows_all, brick_edge, pairs_z, channels):
    result = jnp.zeros((rows_all, brick_edge, brick_edge, pairs_z, 2 * channels), jnp.float32)
    for row_offset in range(3):
        for col_offset in range(3):
            window_part = windows[
                :, row_offset : row_offset + brick_edge, col_offset : col_offset + brick_edge
            ]
            result = result + jnp.einsum(
                "nabjk,kc->nabjc",
                window_part,
                banded[row_offset, col_offset],
                preferred_element_type=jnp.float32,
            )
    return result


def body(features, cotangent, kernel, neighbours):
    realizations = features.shape[0]
    bricks = features.shape[1]
    brick_edge = features.shape[2]
    channels = kernel.shape[-1]
    rows_all = realizations * bricks
    tile_stride = TILES_Y
    pairs_z = brick_edge // 2
    position = lax.axis_index("space")
    neighbour_slots = neighbours.reshape(rows_all, 6)
    present = neighbour_slots >= 0
    safe_links = jnp.where(present, neighbour_slots, 0)
    source_device = safe_links // bricks
    base_rows = jnp.repeat(jnp.arange(realizations, dtype=jnp.int32) * bricks, bricks)[:, None]
    flat_slot = base_rows + safe_links % bricks

    def select(tables, shifts, column):
        return choose_rows(tables, shifts, column, source_device, flat_slot, present, position)

    volume = features.reshape(rows_all, brick_edge, brick_edge, brick_edge * channels)
    upper_face = volume[:, brick_edge - 1]
    lower_face = volume[:, 0]
    from_below = shifted(upper_face, "space", tile_stride)
    from_above = shifted(lower_face, "space", -tile_stride)
    below_part = select([upper_face, from_below], [0, -tile_stride], 0)
    above_part = select([lower_face, from_above], [0, tile_stride], 1)
    layered_x = jnp.concatenate([below_part[:, None], volume, above_part[:, None]], axis=1)
    upper_face = layered_x[:, :, brick_edge - 1]
    lower_face = layered_x[:, :, 0]
    from_below = shifted(upper_face, "space", 1)
    from_above = shifted(lower_face, "space", -1)
    below_part = select([upper_face, from_below], [0, -1], 2)
    above_part = select([lower_face, from_above], [0, 1], 3)
    layered_y = jnp.concatenate([below_part[:, :, None], layered_x, above_part[:, :, None]], axis=2)
    upper_face = layered_y[..., (brick_edge - 1) * channels :]
    lower_face = layered_y[..., :channels]
    extended = jnp.concatenate(
        [select([upper_face], [0], 4), layered_y, select([lower_face], [0], 5)], axis=-1
    )
    banded = make_banded(kernel, channels)
    windows = make_windows(extended, channels, pairs_z)
    result = correlate(windows, banded, rows_all, brick_edge, pairs_z, channels)
    response = result.reshape(features.shape).astype(jnp.bfloat16)
    cotangent_pairs = cotangent.reshape(rows_all, brick_edge, brick_edge, pairs_z, 2 * channels)
    band_terms = []
    for row_offset in range(3):
        for col_offset in range(3):
            window_part = windows[
                :, row_offset : row_offset + brick_edge, col_offset : col_offset + brick_edge
            ]
            band_terms.append(
                jnp.einsum(
                    "nabjk,nabjc->kc",
                    window_part,
                    cotangent_pairs,
                    preferred_element_type=jnp.float32,
                )
            )
    band_grad = jnp.stack(band_terms).reshape(3, 3, 4, channels, 2, channels)
    kernel_local = jnp.stack(
        [
            band_grad[:, :, tap_z, :, 0, :] + band_grad[:, :, tap_z + 1, :, 1, :]
            for tap_z in range(3)
        ],
        axis=2,
    )
    cells_all = rows_all * lax.axis_size("dp") * lax.axis_size("space") * brick_edge**3
    factor = 1.0 / math.sqrt(cells_all)
    kernel_grad = lax.psum(kernel_local, ("space", "dp")) * factor
    spread = jnp.zeros(
        (rows_all, brick_edge + 2, brick_edge + 2, pairs_z, 4 * channels), jnp.float32
    )
    for row_offset in range(3):
        for col_offset in range(3):
            contribution = jnp.einsum(
                "nabjc,kc->nabjk",
                cotangent_pairs,
                banded[row_offset, col_offset],
                preferred_element_type=jnp.float32,
            )
            spread = spread.at[
                :, row_offset : row_offset + brick_edge, col_offset : col_offset + brick_edge
            ].add(contribution)
    widened = jnp.zeros(
        (rows_all, brick_edge + 2, brick_edge + 2, (brick_edge + 2) * channels), jnp.float32
    )
    for block_index in range(pairs_z):
        widened = widened.at[
            ..., 2 * channels * block_index : 2 * channels * block_index + 4 * channels
        ].add(spread[..., block_index, :])
    lower_rim = widened[..., :channels]
    upper_rim = widened[..., (brick_edge + 1) * channels :]
    trimmed_z = widened[..., channels : (brick_edge + 1) * channels]
    trimmed_z = trimmed_z.at[..., (brick_edge - 1) * channels :].add(select([lower_rim], [0], 5))
    trimmed_z = trimmed_z.at[..., :channels].add(select([upper_rim], [0], 4))
    lower_rim = trimmed_z[:, :, 0]
    upper_rim = trimmed_z[:, :, brick_edge + 1]
    trimmed_y = trimmed_z[:, :, 1 : brick_edge + 1]
    from_below = shifted(upper_rim.astype(jnp.bfloat16), "space", 1).astype(upper_rim.dtype)
    from_above = shifted(lower_rim.astype(jnp.bfloat16), "space", -1).astype(lower_rim.dtype)
    trimmed_y = trimmed_y.at[:, :, brick_edge - 1].add(select([lower_rim, from_above], [0, 1], 3))
    trimmed_y = trimmed_y.at[:, :, 0].add(select([upper_rim, from_below], [0, -1], 2))
    lower_rim = trimmed_y[:, 0]
    upper_rim = trimmed_y[:, brick_edge + 1]
    trimmed_x = trimmed_y[:, 1 : brick_edge + 1]
    from_below = shifted(upper_rim.astype(jnp.bfloat16), "space", tile_stride).astype(
        upper_rim.dtype
    )
    from_above = shifted(lower_rim.astype(jnp.bfloat16), "space", -tile_stride).astype(
        lower_rim.dtype
    )
    trimmed_x = trimmed_x.at[:, brick_edge - 1].add(
        select([lower_rim, from_above], [0, tile_stride], 1)
    )
    trimmed_x = trimmed_x.at[:, 0].add(select([upper_rim, from_below], [0, -tile_stride], 0))
    feature_grad = trimmed_x.reshape(features.shape).astype(jnp.bfloat16)
    return (response, feature_grad, kernel_grad)


def solution(mesh):
    in_specs = (
        P(("groups", "dp"), "space", None, None, None),
        P(("groups", "dp"), "space", None, None, None),
        P(),
        P(("groups", "dp"), "space", None),
    )
    out_specs = (
        P(("groups", "dp"), "space", None, None, None),
        P(("groups", "dp"), "space", None, None, None),
        P("groups", None, None, None, None),
    )
    return jax.shard_map(body, mesh=mesh, in_specs=in_specs, out_specs=out_specs, check_vma=False)
```

profile of v0, /device:TPU:0, one launch (start us, length us, event | category | flops | bytes accessed | tf_op | source)
XLA Modules:
  0.0 196.4 jit_solution(7922815339144183871)
XLA Ops:
  8.0 5.9 %collective-permute-start = (bf16[2,8,512]{2,1,0:T(8,128)(2,1)S(1)}, bf16[2,8,512]{2,1,0:T(8,128)(2,1)S(1)}, u32[]{:S(2)}, u32[]{:S(2)}) collective-permute-start(bf16[2,8,512]{2,1,0:T(8,128)(2,1)S(1)} %get-tuple-element.377), channel_id=1, source_target_pairs={{0,8},{2,10},{4,12},{6,14},{1,9},{3,11},{5,13},{7,15},{16,24},{18,... | collective-permute-start | bytes 49160 | tf_op jit(solution)/shard_map/ppermute | solution.py:13
  14.0 1.3 collective-permute-start.1
  19.5 1.2 copy.377
  22.5 1.5 fusion.10
  24.0 2.8 %scatter-add.65 = f32[2,10,10,4,256]{4,2,1,0,3:T(8,128)S(1)} dynamic-update-slice(f32[2,10,10,4,256]{4,2,1,0,3:T(8,128)S(1)} %scatter-add.64, f32[2,8,8,4,256]{4,2,1,0,3:T(8,128)S(1)} %fusion.10, s32[]{:T(128)} %constant.794.clone.1, s32[]{:T(128)} %bitcast.54, s32[]{:T(128)} %bitcast.55, s32[]{:T(128)} %constant.794.clone.1, s32[]{:T(128)} %constant.794.clone.1) | dynamic-update-slice | bytes 1048580 | tf_op jit(solution)/shard_map/scatter-add | solution.py:144
  26.9 2.1 %fusion.9 = f32[2,8,8,4,256]{4,2,1,0,3:T(8,128)S(1)} fusion(f32[2,10,10,4,256]{4,2,1,0,3:T(8,128)S(1)} %scatter-add.65, s32[]{:T(128)} %bitcast.59, s32[]{:T(128)} %bitcast.60, pred[]{:T(512)} %and_reduce_fusion, bf16[3,3,256,128]{3,2,1,0:T(8,128)(2,1)S(1)} %reshape.1187, bf16[1,2,8,8,512]{4,3,2,1,0:T(8,128)(2,1)S(1)} %copy-done), kind=kOutput, calls=%fused_computation.28 | convolution fusion | flops 33816576 | bytes 1245193 | tf_op jit(solution)/shard_map/nabjc,kc->nabjk/dot_general | solution.py:136
  29.0 2.9 %scatter-add.66 = f32[2,10,10,4,256]{4,2,1,0,3:T(8,128)S(1)} dynamic-update-slice(f32[2,10,10,4,256]{4,2,1,0,3:T(8,128)S(1)} %scatter-add.65, f32[2,8,8,4,256]{4,2,1,0,3:T(8,128)S(1)} %fusion.9, s32[]{:T(128)} %constant.794.clone.1, s32[]{:T(128)} %bitcast.59, s32[]{:T(128)} %bitcast.60, s32[]{:T(128)} %constant.794.clone.1, s32[]{:T(128)} %constant.794.clone.1) | dynamic-update-slice | bytes 1048580 | tf_op jit(solution)/shard_map/scatter-add | solution.py:144
  32.4 1.5 scatter-add.70
  34.2 1.5 scatter-add.71
  36.3 1.5 scatter-add.75
  38.0 1.5 scatter-add.76
  41.7 3.1 %scatter-add.85 = f32[2,10,10,512]{3,2,1,0:T(8,128)S(1)} dynamic-update-slice(f32[2,10,10,512]{3,2,1,0:T(8,128)S(1)} %slice.1260, f32[2,10,10,64]{3,2,1,0:T(8,128)S(1)} %get-tuple-element.368, s32[]{:T(128)} %constant.794.clone.1, s32[]{:T(128)} %constant.794.clone.1, s32[]{:T(128)} %constant.794.clone.1, s32[]{:T(128)} %constant.811.clone.1) | dynamic-update-slice | bytes 102404 | tf_op jit(solution)/shard_map/scatter-add | solution.py:155
  45.6 1.3 collective-permute-start.4
  46.9 4.5 %collective-permute-start.5 = (bf16[2,10,512]{2,0,1:T(2,128)(2,1)S(1)}, bf16[2,10,512]{2,0,1:T(2,128)(2,1)S(1)}, u32[]{:S(2)}, u32[]{:S(2)}) collective-permute-start(bf16[2,10,512]{2,0,1:T(2,128)(2,1)S(1)} %bitcast.421), channel_id=1, source_target_pairs={{0,2},{2,4},{4,6},{6,8},{8,10},{10,12},{12,14},{1,3},{3,5},{5,7},{... | collective-permute-start | bytes 61448 | tf_op jit(solution)/shard_map/ppermute | solution.py:13
  53.2 1.3 collective-permute-start.3
  54.5 4.9 %collective-permute-start.2 = (bf16[2,10,512]{2,1,0:T(8,128)(2,1)S(1)}, bf16[2,10,512]{2,1,0:T(8,128)(2,1)S(1)}, u32[]{:S(2)}, u32[]{:S(2)}) collective-permute-start(bf16[2,10,512]{2,1,0:T(8,128)(2,1)S(1)} %copy.364), channel_id=1, source_target_pairs={{0,2},{2,4},{4,6},{6,8},{8,10},{10,12},{12,14},{1,3},{3,5},{5,7},{... | collective-permute-start | bytes 61448 | tf_op jit(solution)/shard_map/ppermute | solution.py:13
  61.4 5.4 %collective-permute-start.7 = (bf16[2,8,512]{2,1,0:T(8,128)(2,1)S(1)}, bf16[2,8,512]{2,1,0:T(8,128)(2,1)S(1)}, u32[]{:S(2)}, u32[]{:S(2)}) collective-permute-start(bf16[2,8,512]{2,1,0:T(8,128)(2,1)S(1)} %get-tuple-element.365), channel_id=1, source_target_pairs={{0,8},{2,10},{4,12},{6,14},{1,9},{3,11},{5,13},{7,15},{16,24},{18,... | collective-permute-start | bytes 49160 | tf_op jit(solution)/shard_map/ppermute | solution.py:13
  66.9 1.5 collective-permute-start.6
  72.3 1.4 fusion.129
  78.4 0.9 fusion.20
  79.4 0.9 fusion.19
  80.3 0.9 fusion.18
  81.3 0.9 fusion.17
  83.2 0.9 fusion.15
  84.1 0.9 fusion.14
  85.0 0.9 fusion.13
  85.9 2.7 %reshape.1202 = f32[3,3,4,64,2,64]{5,4,3,2,1,0:T(2,128)S(1)} reshape(f32[9,256,128]{2,1,0:T(8,128)} %fusion.13) | data formatting | bytes 2359296 | tf_op jit(solution)/shard_map/reshape | solution.py:120
  88.6 1.9 fusion.128
  90.7 1.0 pad_maximum_fusion
  91.7 1.7 fusion.12
  93.4 94.0 %all-reduce.5.cloned.1.call-done = f32[3,3,3,64,64]{4,3,2,1,0:T(8,128)} async-done(((f32[3,3,3,64,64]{4,3,2,1,0:T(8,128)}), f32[3,3,3,64,64]{4,3,2,1,0:T(8,128)}) %all-reduce.5.cloned.1.call-update) | async-done | bytes 442384 | tf_op jit(solution)/shard_map/psum | solution.py:130
  187.4 2.2 %broadcast_multiply_fusion = f32[3,3,3,64,64]{4,3,2,1,0:T(8,128)} fusion(f32[3,3,3,64,64]{4,3,2,1,0:T(8,128)} %all-reduce.5.cloned.1.call-done), kind=kLoop, calls=%fused_computation.62 | loop fusion | flops 110592 | bytes 884736 | tf_op jit(solution)/shard_map/mul | solution.py:130
  (162 shorter events, 24.0 us)
Async XLA Ops:
  7.2 14.9 %copy-start = (bf16[1,2,8,8,512]{4,3,2,1,0:T(8,128)(2,1)S(1)}, bf16[1,2,8,8,512]{4,3,2,1,0:T(8,128)(2,1)}, u32[]{:S(2)}) copy-start(bf16[1,2,8,8,512]{4,3,2,1,0:T(8,128)(2,1)} %param.67) | copy-start | bytes 393220
  7.2 12.2 %copy-start.2 = (bf16[3,3,3,64,64]{4,3,2,1,0:T(8,128)(2,1)S(1)}, bf16[3,3,3,64,64]{4,3,2,1,0:T(8,128)(2,1)}, u32[]{:S(2)}) copy-start(bf16[3,3,3,64,64]{4,3,2,1,0:T(8,128)(2,1)} %param.68) | copy-start | bytes 663556
  7.2 180.2 %all-reduce.5.cloned.1.call-start = ((), (), s32[]{:S(2)}) async-start(), calls=%async_computation | async-start | bytes 1769472 | tf_op jit(solution)/shard_map/psum | solution.py:130
  8.0 43.7 %collective-permute-start = (bf16[2,8,512]{2,1,0:T(8,128)(2,1)S(1)}, bf16[2,8,512]{2,1,0:T(8,128)(2,1)S(1)}, u32[]{:S(2)}, u32[]{:S(2)}) collective-permute-start(bf16[2,8,512]{2,1,0:T(8,128)(2,1)S(1)} %get-tuple-element.377), channel_id=1, source_target_pairs={{0,8},{2,10},{4,12},{6,14},{1,9},{3,11},{5,13},{7,15},{16,24},{18,... | collective-permute-start | bytes 49160 | tf_op jit(solution)/shard_map/ppermute | solution.py:13
  14.0 38.3 %collective-permute-start.1 = (bf16[2,8,512]{2,1,0:T(8,128)(2,1)S(1)}, bf16[2,8,512]{2,1,0:T(8,128)(2,1)S(1)}, u32[]{:S(2)}, u32[]{:S(2)}) collective-permute-start(bf16[2,8,512]{2,1,0:T(8,128)(2,1)S(1)} %get-tuple-element.378), channel_id=1, source_target_pairs={{8,0},{10,2},{12,4},{14,6},{9,1},{11,3},{13,5},{15,7},{24,16},{26,... | collective-permute-start | bytes 49160 | tf_op jit(solution)/shard_map/ppermute | solution.py:13
  20.7 0.7 copy-start.10
  21.4 53.8 %copy-start.1 = (bf16[3,3,256,128]{3,2,1,0:T(8,128)(2,1)}, bf16[3,3,256,128]{3,2,1,0:T(8,128)(2,1)S(1)}, u32[]{:S(2)}) copy-start(bf16[3,3,256,128]{3,2,1,0:T(8,128)(2,1)S(1)} %reshape.1187) | copy-start | bytes 1769476
  44.9 8.1 %copy-start.3 = (bf16[1,2,8,8,512]{4,3,2,1,0:T(8,128)(2,1)S(1)}, bf16[1,2,8,8,512]{4,3,2,1,0:T(8,128)(2,1)}, u32[]{:S(2)}) copy-start(bf16[1,2,8,8,512]{4,3,2,1,0:T(8,128)(2,1)} %param.66) | copy-start | bytes 393220
  45.6 13.9 %collective-permute-start.4 = (bf16[2,10,512]{2,0,1:T(2,128)(2,1)S(1)}, bf16[2,10,512]{2,0,1:T(2,128)(2,1)S(1)}, u32[]{:S(2)}, u32[]{:S(2)}) collective-permute-start(bf16[2,10,512]{2,0,1:T(2,128)(2,1)S(1)} %bitcast.420), channel_id=1, source_target_pairs={{2,0},{4,2},{6,4},{8,6},{10,8},{12,10},{14,12},{3,1},{5,3},{7,5},{... | collective-permute-start | bytes 61448 | tf_op jit(solution)/shard_map/ppermute | solution.py:13
  46.9 12.5 %collective-permute-start.5 = (bf16[2,10,512]{2,0,1:T(2,128)(2,1)S(1)}, bf16[2,10,512]{2,0,1:T(2,128)(2,1)S(1)}, u32[]{:S(2)}, u32[]{:S(2)}) collective-permute-start(bf16[2,10,512]{2,0,1:T(2,128)(2,1)S(1)} %bitcast.421), channel_id=1, source_target_pairs={{0,2},{2,4},{4,6},{6,8},{8,10},{10,12},{12,14},{1,3},{3,5},{5,7},{... | collective-permute-start | bytes 61448 | tf_op jit(solution)/shard_map/ppermute | solution.py:13
  53.2 15.2 %collective-permute-start.3 = (bf16[2,10,512]{2,1,0:T(8,128)(2,1)S(1)}, bf16[2,10,512]{2,1,0:T(8,128)(2,1)S(1)}, u32[]{:S(2)}, u32[]{:S(2)}) collective-permute-start(bf16[2,10,512]{2,1,0:T(8,128)(2,1)S(1)} %copy.368), channel_id=1, source_target_pairs={{2,0},{4,2},{6,4},{8,6},{10,8},{12,10},{14,12},{3,1},{5,3},{7,5},{... | collective-permute-start | bytes 61448 | tf_op jit(solution)/shard_map/ppermute | solution.py:13
  54.5 14.6 %collective-permute-start.2 = (bf16[2,10,512]{2,1,0:T(8,128)(2,1)S(1)}, bf16[2,10,512]{2,1,0:T(8,128)(2,1)S(1)}, u32[]{:S(2)}, u32[]{:S(2)}) collective-permute-start(bf16[2,10,512]{2,1,0:T(8,128)(2,1)S(1)} %copy.364), channel_id=1, source_target_pairs={{0,2},{2,4},{4,6},{6,8},{8,10},{10,12},{12,14},{1,3},{3,5},{5,7},{... | collective-permute-start | bytes 61448 | tf_op jit(solution)/shard_map/ppermute | solution.py:13
  61.4 14.0 %collective-permute-start.7 = (bf16[2,8,512]{2,1,0:T(8,128)(2,1)S(1)}, bf16[2,8,512]{2,1,0:T(8,128)(2,1)S(1)}, u32[]{:S(2)}, u32[]{:S(2)}) collective-permute-start(bf16[2,8,512]{2,1,0:T(8,128)(2,1)S(1)} %get-tuple-element.365), channel_id=1, source_target_pairs={{0,8},{2,10},{4,12},{6,14},{1,9},{3,11},{5,13},{7,15},{16,24},{18,... | collective-permute-start | bytes 49160 | tf_op jit(solution)/shard_map/ppermute | solution.py:13
  66.9 9.1 %collective-permute-start.6 = (bf16[2,8,512]{2,1,0:T(8,128)(2,1)S(1)}, bf16[2,8,512]{2,1,0:T(8,128)(2,1)S(1)}, u32[]{:S(2)}, u32[]{:S(2)}) collective-permute-start(bf16[2,8,512]{2,1,0:T(8,128)(2,1)S(1)} %get-tuple-element.366), channel_id=1, source_target_pairs={{8,0},{10,2},{12,4},{14,6},{9,1},{11,3},{13,5},{15,7},{24,16},{26,... | collective-permute-start | bytes 49160 | tf_op jit(solution)/shard_map/ppermute | solution.py:13
  75.4 2.1 %copy-start.9 = (bf16[2,8,8,4,256]{4,2,3,1,0:T(8,128)(2,1)S(1)}, bf16[2,8,8,4,256]{4,2,3,1,0:T(8,128)(2,1)}, u32[]{:S(2)}) copy-start(bf16[2,8,8,4,256]{4,2,3,1,0:T(8,128)(2,1)} %get-tuple-element.360) | copy-start | bytes 786436
  77.5 1.0 copy-start.8
  78.4 0.9 copy-start.7
  79.4 0.9 copy-start.6
  80.3 0.9 copy-start.5
  81.3 0.9 copy-start.4
Sparse Core Ops, SparseCore 0:
  91.8 95.5 all-reduce.4
where the time goes:
time: 197 us; the launch traced here: 196 us
  waiting for transfers between devices  94 us (48%)
  local copies, waits for them, and re-layouts  35.9 us (18%)
  starting transfers between devices  26.2 us (13%)
  matrix products  17.3 us (9%)
  between operations  15.1 us (8%)
  other arithmetic  7.91 us (4%)
    psum x1, waiting for transfers between devices, body(): kernel_grad = lax.psum(kernel_local, ('space', 'dp')) * factor  94 us
    ppermute x8, starting transfers between devices, shifted(): return lax.ppermute(x, axis, pairs)  26.2 us
    scatter-add x7, local copies, waits for them, and re-layouts, body(): spread = spread.at[:, row_offset:row_offset + brick_edge, col_offset:col_...  12 us
    dot_general x9, matrix products, body(): jnp.einsum('nabjk,nabjc->kc', window_part, cotangent_pairs, preferred_ele...  8.32 us
    gather x12, local copies, waits for them, and re-layouts, choose_rows(): picked = jnp.take(stacked, row_index, axis=0)  6.66 us
    dot_general x9, matrix products, body(): jnp.einsum('nabjc,kc->nabjk', cotangent_pairs, banded[row_offset, col_off...  5.35 us
  transfers between devices with their start and end apart: 9, of which 1 were waited for; matrix products, arithmetic and copies ran while one was open for 22% of the time, Pallas kernels for 0%

commit v1 on v0

--- a/solution.py
+++ b/solution.py
@@ -5,6 +5,7 @@
 from jax.sharding import PartitionSpec as P
 
 TILES_Y = 4
+cells_end = lambda obj: jax.lax.psum(jax.lax.psum(obj, axis_name="dp"), axis_name="space")
 
 
 def shifted(x, axis, by):
@@ -127,7 +128,7 @@
     )
     cells_all = rows_all * lax.axis_size("dp") * lax.axis_size("space") * brick_edge**3
     factor = 1.0 / math.sqrt(cells_all)
-    kernel_grad = lax.psum(kernel_local, ("space", "dp")) * factor
+    kernel_grad = cells_end(kernel_local) * factor
     spread = jnp.zeros(
         (rows_all, brick_edge + 2, brick_edge + 2, pairs_z, 4 * channels), jnp.float32
     )

time: 197 us -> 204 us (1.036)
  waiting for transfers between devices: 94 us -> 97.6 us
  matrix products: 17.3 us -> 19.8 us
    psum x1 -> x2, waiting for transfers between devices: 94 us -> 97.6 us  [the longest x1 77.6 us: jax.lax.psum(jax.lax.psum(obj, axis_name='dp'), axis_name='space')]
    dot_general x9, matrix products: 3.63 us -> 6.15 us  [correlate(): jnp.einsum('nabjk,kc->nabjc', window_part, banded[row_offset, col_offset]...]
  transfers between devices with their start and end apart: 9 -> 10, of which waited for: 1 -> 2; matrix products, arithmetic and copies ran while one was open for 22% -> 22% of each run, Pallas kernels for 0% -> 0%
where the time goes in v1:
time: 204 us; the launch traced here: 203 us
  waiting for transfers between devices  97.6 us (48%)
  local copies, waits for them, and re-layouts  36 us (18%)
  starting transfers between devices  26.3 us (13%)
  matrix products  19.8 us (10%)
  between operations  15.1 us (7%)
  other arithmetic  7.93 us (4%)
    psum x1, waiting for transfers between devices, jax.lax.psum(jax.lax.psum(obj, axis_name='dp'), axis_name='space')  77.6 us
    ppermute x8, starting transfers between devices, shifted(): return lax.ppermute(x, axis, pairs)  26.2 us
    psum x1, waiting for transfers between devices, jax.lax.psum(obj, axis_name='dp')  19.9 us
    scatter-add x7, local copies, waits for them, and re-layouts, body(): spread = spread.at[:, row_offset:row_offset + brick_edge, col_offset:col_...  12 us
    dot_general x9, matrix products, body(): jnp.einsum('nabjk,nabjc->kc', window_part, cotangent_pairs, preferred_ele...  8.3 us
    gather x12, local copies, waits for them, and re-layouts, choose_rows(): picked = jnp.take(stacked, row_index, axis=0)  6.66 us
    dot_general x9, matrix products, correlate(): jnp.einsum('nabjk,kc->nabjc', window_part, banded[row_offset, col_offset]...  6.15 us
    dot_general x9, matrix products, body(): jnp.einsum('nabjc,kc->nabjk', cotangent_pairs, banded[row_offset, col_off...  5.34 us
  transfers between devices with their start and end apart: 10, of which 2 were waited for; matrix products, arithmetic and copies ran while one was open for 22% of the time, Pallas kernels for 0%

profile of v1, /device:TPU:0, one launch (start us, length us, event | category | flops | bytes accessed | tf_op | source)
XLA Modules:
  0.0 202.7 jit_solution(7210605704151709471)
XLA Ops:
  8.0 5.9 %collective-permute-start = (bf16[2,8,512]{2,1,0:T(8,128)(2,1)S(1)}, bf16[2,8,512]{2,1,0:T(8,128)(2,1)S(1)}, u32[]{:S(2)}, u32[]{:S(2)}) collective-permute-start(bf16[2,8,512]{2,1,0:T(8,128)(2,1)S(1)} %get-tuple-element.377), channel_id=1, source_target_pairs={{0,8},{2,10},{4,12},{6,14},{1,9},{3,11},{5,13},{7,15},{16,24},{18,... | collective-permute-start | bytes 49160 | tf_op jit(solution)/shard_map/ppermute | solution.py:14
  14.0 1.3 collective-permute-start.1
  19.5 1.2 copy.377
  22.5 1.5 fusion.10
  24.0 2.8 %scatter-add.65 = f32[2,10,10,4,256]{4,2,1,0,3:T(8,128)S(1)} dynamic-update-slice(f32[2,10,10,4,256]{4,2,1,0,3:T(8,128)S(1)} %scatter-add.64, f32[2,8,8,4,256]{4,2,1,0,3:T(8,128)S(1)} %fusion.10, s32[]{:T(128)} %constant.794.clone.1, s32[]{:T(128)} %bitcast.54, s32[]{:T(128)} %bitcast.55, s32[]{:T(128)} %constant.794.clone.1, s32[]{:T(128)} %constant.794.clone.1) | dynamic-update-slice | bytes 1048580 | tf_op jit(solution)/shard_map/scatter-add | solution.py:145
  26.9 2.1 %fusion.9 = f32[2,8,8,4,256]{4,2,1,0,3:T(8,128)S(1)} fusion(f32[2,10,10,4,256]{4,2,1,0,3:T(8,128)S(1)} %scatter-add.65, s32[]{:T(128)} %bitcast.59, s32[]{:T(128)} %bitcast.60, pred[]{:T(512)} %and_reduce_fusion, bf16[3,3,256,128]{3,2,1,0:T(8,128)(2,1)S(1)} %reshape.1187, bf16[1,2,8,8,512]{4,3,2,1,0:T(8,128)(2,1)S(1)} %copy-done), kind=kOutput, calls=%fused_computation.28 | convolution fusion | flops 33816576 | bytes 1245193 | tf_op jit(solution)/shard_map/nabjc,kc->nabjk/dot_general | solution.py:137
  29.0 2.9 %scatter-add.66 = f32[2,10,10,4,256]{4,2,1,0,3:T(8,128)S(1)} dynamic-update-slice(f32[2,10,10,4,256]{4,2,1,0,3:T(8,128)S(1)} %scatter-add.65, f32[2,8,8,4,256]{4,2,1,0,3:T(8,128)S(1)} %fusion.9, s32[]{:T(128)} %constant.794.clone.1, s32[]{:T(128)} %bitcast.59, s32[]{:T(128)} %bitcast.60, s32[]{:T(128)} %constant.794.clone.1, s32[]{:T(128)} %constant.794.clone.1) | dynamic-update-slice | bytes 1048580 | tf_op jit(solution)/shard_map/scatter-add | solution.py:145
  32.4 1.5 scatter-add.70
  34.2 1.5 scatter-add.71
  36.2 1.5 scatter-add.75
  38.0 1.5 scatter-add.76
  41.7 3.1 %scatter-add.85 = f32[2,10,10,512]{3,2,1,0:T(8,128)S(1)} dynamic-update-slice(f32[2,10,10,512]{3,2,1,0:T(8,128)S(1)} %slice.1260, f32[2,10,10,64]{3,2,1,0:T(8,128)S(1)} %get-tuple-element.368, s32[]{:T(128)} %constant.794.clone.1, s32[]{:T(128)} %constant.794.clone.1, s32[]{:T(128)} %constant.794.clone.1, s32[]{:T(128)} %constant.811.clone.1) | dynamic-update-slice | bytes 102404 | tf_op jit(solution)/shard_map/scatter-add | solution.py:156
  45.6 1.3 collective-permute-start.4
  46.9 4.5 %collective-permute-start.5 = (bf16[2,10,512]{2,0,1:T(2,128)(2,1)S(1)}, bf16[2,10,512]{2,0,1:T(2,128)(2,1)S(1)}, u32[]{:S(2)}, u32[]{:S(2)}) collective-permute-start(bf16[2,10,512]{2,0,1:T(2,128)(2,1)S(1)} %bitcast.421), channel_id=1, source_target_pairs={{0,2},{2,4},{4,6},{6,8},{8,10},{10,12},{12,14},{1,3},{3,5},{5,7},{... | collective-permute-start | bytes 61448 | tf_op jit(solution)/shard_map/ppermute | solution.py:14
  53.1 1.3 collective-permute-start.3
  54.4 4.9 %collective-permute-start.2 = (bf16[2,10,512]{2,1,0:T(8,128)(2,1)S(1)}, bf16[2,10,512]{2,1,0:T(8,128)(2,1)S(1)}, u32[]{:S(2)}, u32[]{:S(2)}) collective-permute-start(bf16[2,10,512]{2,1,0:T(8,128)(2,1)S(1)} %copy.364), channel_id=1, source_target_pairs={{0,2},{2,4},{4,6},{6,8},{8,10},{10,12},{12,14},{1,3},{3,5},{5,7},{... | collective-permute-start | bytes 61448 | tf_op jit(solution)/shard_map/ppermute | solution.py:14
  61.4 5.4 %collective-permute-start.7 = (bf16[2,8,512]{2,1,0:T(8,128)(2,1)S(1)}, bf16[2,8,512]{2,1,0:T(8,128)(2,1)S(1)}, u32[]{:S(2)}, u32[]{:S(2)}) collective-permute-start(bf16[2,8,512]{2,1,0:T(8,128)(2,1)S(1)} %get-tuple-element.365), channel_id=1, source_target_pairs={{0,8},{2,10},{4,12},{6,14},{1,9},{3,11},{5,13},{7,15},{16,24},{18,... | collective-permute-start | bytes 49160 | tf_op jit(solution)/shard_map/ppermute | solution.py:14
  66.9 1.5 collective-permute-start.6
  72.3 1.5 fusion.129
  79.7 0.9 fusion.18
  82.6 0.9 fusion.15
  84.4 0.9 fusion.13
  85.4 2.7 %reshape.1202 = f32[3,3,4,64,2,64]{5,4,3,2,1,0:T(2,128)S(1)} reshape(f32[9,256,128]{2,1,0:T(8,128)} %fusion.13) | data formatting | bytes 2359296 | tf_op jit(solution)/shard_map/reshape | solution.py:121
  88.0 1.9 fusion.128
  90.1 1.0 pad_maximum_fusion
  91.1 1.1 convolution_add_fusion.3
  92.2 1.1 convolution_add_fusion.2
  93.3 19.9 %all-reduce.6.cloned.1.call-done = f32[3,3,3,64,64]{4,3,2,1,0:T(8,128)} async-done(((f32[3,3,3,64,64]{4,3,2,1,0:T(8,128)}), f32[3,3,3,64,64]{4,3,2,1,0:T(8,128)}) %all-reduce.6.cloned.1.call-update) | async-done | bytes 442384 | tf_op jit(solution)/shard_map/psum | solution.py:8
  113.2 1.1 convolution_add_fusion.1
  114.3 1.7 fusion.12
  116.1 77.6 %all-reduce.8.cloned.1.call-done = f32[3,3,3,64,64]{4,3,2,1,0:T(8,128)} async-done(((f32[3,3,3,64,64]{4,3,2,1,0:T(8,128)}), f32[3,3,3,64,64]{4,3,2,1,0:T(8,128)}) %all-reduce.8.cloned.1.call-update) | async-done | bytes 442384 | tf_op jit(solution)/shard_map/psum | solution.py:8
  193.7 2.2 %broadcast_multiply_fusion = f32[3,3,3,64,64]{4,3,2,1,0:T(8,128)} fusion(f32[3,3,3,64,64]{4,3,2,1,0:T(8,128)} %all-reduce.8.cloned.1.call-done), kind=kLoop, calls=%fused_computation.62 | loop fusion | flops 110592 | bytes 884736 | tf_op jit(solution)/shard_map/mul | solution.py:131
  (169 shorter events, 27.1 us)
Async XLA Ops:
  7.2 14.9 %copy-start = (bf16[1,2,8,8,512]{4,3,2,1,0:T(8,128)(2,1)S(1)}, bf16[1,2,8,8,512]{4,3,2,1,0:T(8,128)(2,1)}, u32[]{:S(2)}) copy-start(bf16[1,2,8,8,512]{4,3,2,1,0:T(8,128)(2,1)} %param.67) | copy-start | bytes 393220
  7.2 12.2 %copy-start.2 = (bf16[3,3,3,64,64]{4,3,2,1,0:T(8,128)(2,1)S(1)}, bf16[3,3,3,64,64]{4,3,2,1,0:T(8,128)(2,1)}, u32[]{:S(2)}) copy-start(bf16[3,3,3,64,64]{4,3,2,1,0:T(8,128)(2,1)} %param.68) | copy-start | bytes 663556
  7.2 106.0 %all-reduce.6.cloned.1.call-start = ((), (), s32[]{:S(2)}) async-start(), calls=%async_computation | async-start | bytes 1769472 | tf_op jit(solution)/shard_map/psum | solution.py:8
  8.0 43.7 %collective-permute-start = (bf16[2,8,512]{2,1,0:T(8,128)(2,1)S(1)}, bf16[2,8,512]{2,1,0:T(8,128)(2,1)S(1)}, u32[]{:S(2)}, u32[]{:S(2)}) collective-permute-start(bf16[2,8,512]{2,1,0:T(8,128)(2,1)S(1)} %get-tuple-element.377), channel_id=1, source_target_pairs={{0,8},{2,10},{4,12},{6,14},{1,9},{3,11},{5,13},{7,15},{16,24},{18,... | collective-permute-start | bytes 49160 | tf_op jit(solution)/shard_map/ppermute | solution.py:14
  14.0 38.3 %collective-permute-start.1 = (bf16[2,8,512]{2,1,0:T(8,128)(2,1)S(1)}, bf16[2,8,512]{2,1,0:T(8,128)(2,1)S(1)}, u32[]{:S(2)}, u32[]{:S(2)}) collective-permute-start(bf16[2,8,512]{2,1,0:T(8,128)(2,1)S(1)} %get-tuple-element.378), channel_id=1, source_target_pairs={{8,0},{10,2},{12,4},{14,6},{9,1},{11,3},{13,5},{15,7},{24,16},{26,... | collective-permute-start | bytes 49160 | tf_op jit(solution)/shard_map/ppermute | solution.py:14
  20.7 0.7 copy-start.12
  21.4 53.2 %copy-start.1 = (bf16[3,3,256,128]{3,2,1,0:T(8,128)(2,1)}, bf16[3,3,256,128]{3,2,1,0:T(8,128)(2,1)S(1)}, u32[]{:S(2)}) copy-start(bf16[3,3,256,128]{3,2,1,0:T(8,128)(2,1)S(1)} %reshape.1187) | copy-start | bytes 1769476
  44.8 8.1 %copy-start.3 = (bf16[1,2,8,8,512]{4,3,2,1,0:T(8,128)(2,1)S(1)}, bf16[1,2,8,8,512]{4,3,2,1,0:T(8,128)(2,1)}, u32[]{:S(2)}) copy-start(bf16[1,2,8,8,512]{4,3,2,1,0:T(8,128)(2,1)} %param.66) | copy-start | bytes 393220
  45.6 13.9 %collective-permute-start.4 = (bf16[2,10,512]{2,0,1:T(2,128)(2,1)S(1)}, bf16[2,10,512]{2,0,1:T(2,128)(2,1)S(1)}, u32[]{:S(2)}, u32[]{:S(2)}) collective-permute-start(bf16[2,10,512]{2,0,1:T(2,128)(2,1)S(1)} %bitcast.420), channel_id=1, source_target_pairs={{2,0},{4,2},{6,4},{8,6},{10,8},{12,10},{14,12},{3,1},{5,3},{7,5},{... | collective-permute-start | bytes 61448 | tf_op jit(solution)/shard_map/ppermute | solution.py:14
  46.9 12.5 %collective-permute-start.5 = (bf16[2,10,512]{2,0,1:T(2,128)(2,1)S(1)}, bf16[2,10,512]{2,0,1:T(2,128)(2,1)S(1)}, u32[]{:S(2)}, u32[]{:S(2)}) collective-permute-start(bf16[2,10,512]{2,0,1:T(2,128)(2,1)S(1)} %bitcast.421), channel_id=1, source_target_pairs={{0,2},{2,4},{4,6},{6,8},{8,10},{10,12},{12,14},{1,3},{3,5},{5,7},{... | collective-permute-start | bytes 61448 | tf_op jit(solution)/shard_map/ppermute | solution.py:14
  53.1 15.2 %collective-permute-start.3 = (bf16[2,10,512]{2,1,0:T(8,128)(2,1)S(1)}, bf16[2,10,512]{2,1,0:T(8,128)(2,1)S(1)}, u32[]{:S(2)}, u32[]{:S(2)}) collective-permute-start(bf16[2,10,512]{2,1,0:T(8,128)(2,1)S(1)} %copy.368), channel_id=1, source_target_pairs={{2,0},{4,2},{6,4},{8,6},{10,8},{12,10},{14,12},{3,1},{5,3},{7,5},{... | collective-permute-start | bytes 61448 | tf_op jit(solution)/shard_map/ppermute | solution.py:14
  54.4 14.7 %collective-permute-start.2 = (bf16[2,10,512]{2,1,0:T(8,128)(2,1)S(1)}, bf16[2,10,512]{2,1,0:T(8,128)(2,1)S(1)}, u32[]{:S(2)}, u32[]{:S(2)}) collective-permute-start(bf16[2,10,512]{2,1,0:T(8,128)(2,1)S(1)} %copy.364), channel_id=1, source_target_pairs={{0,2},{2,4},{4,6},{6,8},{8,10},{10,12},{12,14},{1,3},{3,5},{5,7},{... | collective-permute-start | bytes 61448 | tf_op jit(solution)/shard_map/ppermute | solution.py:14
  61.4 13.4 %collective-permute-start.7 = (bf16[2,8,512]{2,1,0:T(8,128)(2,1)S(1)}, bf16[2,8,512]{2,1,0:T(8,128)(2,1)S(1)}, u32[]{:S(2)}, u32[]{:S(2)}) collective-permute-start(bf16[2,8,512]{2,1,0:T(8,128)(2,1)S(1)} %get-tuple-element.365), channel_id=1, source_target_pairs={{0,8},{2,10},{4,12},{6,14},{1,9},{3,11},{5,13},{7,15},{16,24},{18,... | collective-permute-start | bytes 49160 | tf_op jit(solution)/shard_map/ppermute | solution.py:14
  66.9 8.5 %collective-permute-start.6 = (bf16[2,8,512]{2,1,0:T(8,128)(2,1)S(1)}, bf16[2,8,512]{2,1,0:T(8,128)(2,1)S(1)}, u32[]{:S(2)}, u32[]{:S(2)}) collective-permute-start(bf16[2,8,512]{2,1,0:T(8,128)(2,1)S(1)} %get-tuple-element.366), channel_id=1, source_target_pairs={{8,0},{10,2},{12,4},{14,6},{9,1},{11,3},{13,5},{15,7},{24,16},{26,... | collective-permute-start | bytes 49160 | tf_op jit(solution)/shard_map/ppermute | solution.py:14
  74.5 2.3 %copy-start.11 = (bf16[2,8,8,4,256]{4,2,3,1,0:T(8,128)(2,1)S(1)}, bf16[2,8,8,4,256]{4,2,3,1,0:T(8,128)(2,1)}, u32[]{:S(2)}) copy-start(bf16[2,8,8,4,256]{4,2,3,1,0:T(8,128)(2,1)} %get-tuple-element.360) | copy-start | bytes 786436
  76.9 1.0 copy-start.10
  77.8 0.9 copy-start.9
  78.8 0.9 copy-start.8
  79.7 0.9 copy-start.7
  80.7 0.9 copy-start.6
  81.6 0.9 copy-start.5
  82.6 0.9 copy-start.4
  91.1 102.6 %all-reduce.8.cloned.1.call-start = ((), (), s32[]{:S(2)}) async-start(), calls=%async_computation.1 | async-start | bytes 1769472 | tf_op jit(solution)/shard_map/psum | solution.py:8
Sparse Core Ops, SparseCore 0:
  91.2 21.9 all-reduce.5
  116.7 76.9 all-reduce.7
